TPU v7x, 32 devices: a whole 2x2x4 slice. The times are simulated.
32 devices in a mesh: sub: 8 (over y, x, core), coarse: 4 (over z).
Axes of the slice: x: 2, y: 2, z: 4, core: 2. Of those that a mesh axis runs over, the one named last changes fastest.
Arguments:
- right_side: float32 [8, 4, 128, 128], P('sub', 'coarse'), may hold values from -150 to 150
- diagonal: float32 [8, 4, 128, 128], P('sub', 'coarse'), may hold values from 2 to 8
- cell_link: float32 [8, 4, 128, 128], P('sub', 'coarse'), may hold values from 0.2 to 0.9
- block_inverse: float32 [8, 4, 128, 128, 128], P('sub', 'coarse'), may hold values from -1 to 1
- coupling: float32 [8, 4, 4, 128, 128], P('sub', 'coarse'), may hold values from -0.26516503 to 0.26516503
- coarse_basis: float32 [8, 4, 128, 128], P('sub', 'coarse'), may hold values from -6 to 6
- coarse_inverse: float32 [512, 512], P('coarse'), may hold values from -0.25 to 0.25
- partner: int32 [8, 4], P('sub'), may hold values from 0 to 7, as said below
- margin_width: int32 [8, 4], P('sub'), may hold values from 4 to 8, as said below
- margin_blocks: int32 [8, 4, 4, 8], P('sub', 'coarse'), may hold values from 0 to 127
- aggregate: int32 [8, 4, 128], P('sub', 'coarse'), may hold values from 0 to 511, as said below
Outputs:
- solution: float32 [8, 4, 128, 128], P('sub', 'coarse')
Inputs may be any that keep to these rules, and one draw needn't show every extreme that they name: partner[s, r] differs from s, partner[partner[s, r], r] = s, and the 4 partners of one subdomain are distinct. margin_width[partner[s, r], r] = margin_width[s, r]; every colour round has a pair with width 8. `margin_blocks`: entries with w >= margin_width[s, r] are not used. aggregate[s, c, b] lies in (s * 4 + c) * 16 to (s * 4 + c + 1) * 16 - 1, and every one of these 16 aggregates has a block of part [s, c].
All inputs are finite; a program needn't handle non-finite values.
Results may differ from a plain program's by a relative error of at most 0.0003.
Values sent between devices are 32-bit elements; how exact they have to be, the bound alone decides.
No kernel may reach another device: no remote copies, remote signals or barrier semaphores. Data moves between devices by JAX's collectives and lax.ppermute only.
A program may use at most 64 MiB of HBM per device.

v0:
```python
import jax
import jax.numpy as jnp
from jax import lax
from jax.sharding import PartitionSpec as P

BS = 128
BPD = 128
AGG_DEV = 16
ITERS = 4


def givens_solve(columns, beta):
    steps_count = len(columns)
    cosines = []
    sines = []
    side_terms = [beta] + [jnp.zeros_like(beta) for unused in range(steps_count)]
    triangle = []
    for column_id in range(steps_count):
        column = list(columns[column_id])
        for row_id in range(column_id):
            upper = column[row_id]
            lower = column[row_id + 1]
            column[row_id] = cosines[row_id] * upper + sines[row_id] * lower
            column[row_id + 1] = cosines[row_id] * lower - sines[row_id] * upper
        upper = column[column_id]
        lower = column[column_id + 1]
        radius = jnp.sqrt(upper * upper + lower * lower)
        cosine = upper / radius
        sine_value = lower / radius
        column[column_id] = radius
        cosines.append(cosine)
        sines.append(sine_value)
        side_terms[column_id + 1] = -sine_value * side_terms[column_id]
        side_terms[column_id] = cosine * side_terms[column_id]
        triangle.append(column)
    weights = [None] * steps_count
    for column_id in reversed(range(steps_count)):
        running = side_terms[column_id]
        for later_col in range(column_id + 1, steps_count):
            running = running - triangle[later_col][column_id] * weights[later_col]
        weights[column_id] = running / triangle[column_id][column_id]
    return weights


def on_device(
    right_side,
    diagonal,
    cell_link,
    block_inverse,
    coupling,
    coarse_basis,
    coarse_inverse,
    partner,
    margin_width,
    margin_blocks,
    aggregate,
):
    highest = lax.Precision.HIGHEST
    block_count = right_side.shape[2]
    unknowns = right_side.shape[3]
    factor = (BS * BPD / AGG_DEV) ** (-0.5)
    inverse_blocks = block_inverse[0, 0]
    couplings = coupling[0, 0]
    basis_local = coarse_basis[0, 0]
    diagonal_local = diagonal[0, 0]
    link_local = cell_link[0, 0]
    paired = partner[0]
    widths = margin_width[0]
    blocks = margin_blocks[0, 0]
    member_of = aggregate[0, 0]
    aggregate_count = coarse_inverse.shape[1]
    member_table = (member_of[:, None] == jnp.arange(aggregate_count)[None, :]).astype(jnp.float32)
    rounds = blocks.shape[0]
    widest = blocks.shape[1]
    target = (blocks.reshape(-1)[:, None] == jnp.arange(block_count)[None, :]).astype(jnp.float32)
    live_mask = (jnp.arange(widest)[None, :] < widths[:, None]).astype(jnp.float32)

    def margin(values):
        outgoing = jnp.take(values, blocks.reshape(-1), axis=0).reshape(rounds, widest, unknowns)
        pieces = []
        for round_id in range(rounds):
            gathered = lax.all_gather(outgoing[round_id], "sub", axis=0, tiled=True)
            pieces.append(lax.dynamic_slice_in_dim(gathered, paired[round_id] * widest, widest, 0))
        incoming = jnp.stack(pieces)
        mapped = (
            jnp.einsum("rij,rwj->rwi", couplings, incoming, precision=highest)
            * live_mask[:, :, None]
        )
        return jnp.einsum(
            "kb,ki->bi", target, mapped.reshape(rounds * widest, unknowns), precision=highest
        )

    def squared_norm(values):
        return lax.psum(jnp.sum(values * values), ("sub", "coarse"))

    start_vector = right_side[0, 0]
    directions = []
    columns = []
    beta = jnp.sqrt(squared_norm(start_vector))
    basis_list = [start_vector / beta]
    for krylov_step in range(ITERS):
        current = basis_list[-1]
        inner = jnp.sum(basis_local * current, axis=1)
        restricted = lax.psum(
            jnp.dot(inner, member_table, precision=highest) * factor, ("sub", "coarse")
        )
        local_part = jnp.einsum(
            "bij,bj->bi", inverse_blocks, current + margin(current), precision=highest
        )
        coarse_part = jnp.dot(coarse_inverse, restricted, precision=highest)
        coarse_full = lax.all_gather(coarse_part, "coarse", axis=0, tiled=True)
        prolonged = jnp.dot(member_table, coarse_full, precision=highest)
        direction = local_part + prolonged[:, None] * basis_local
        directions.append(direction)
        flat_line = direction.reshape(-1)
        link_line = link_local.reshape(-1)
        zero_pad = jnp.zeros((1,), jnp.float32)
        ahead_terms = jnp.concatenate([flat_line[1:], zero_pad]) * link_line
        behind_terms = jnp.concatenate([zero_pad, (link_line * flat_line)[:-1]])
        product = (
            diagonal_local * direction
            - (ahead_terms + behind_terms).reshape(direction.shape)
            - margin(direction)
        )
        projected = lax.psum(
            jnp.stack([jnp.sum(vector * product) for vector in basis_list]), ("sub", "coarse")
        )
        for position in range(len(basis_list)):
            product = product - projected[position] * basis_list[position]
        norm_new = jnp.sqrt(squared_norm(product))
        columns.append([projected[position] for position in range(len(basis_list))] + [norm_new])
        basis_list.append(product / norm_new)
    weights = givens_solve(columns, beta)
    solution = weights[0] * directions[0]
    for position in range(1, ITERS):
        solution = solution + weights[position] * directions[position]
    return solution.reshape(right_side.shape)


def solution(mesh):
    placed = (
        P("sub", "coarse", None, None),
        P("sub", "coarse", None, None),
        P("sub", "coarse", None, None),
        P("sub", "coarse", None, None, None),
        P("sub", "coarse", None, None, None),
        P("sub", "coarse", None, None),
        P("coarse", None),
        P("sub", None),
        P("sub", None),
        P("sub", "coarse", None, None),
        P("sub", "coarse", None),
    )
    return jax.shard_map(
        on_device,
        mesh=mesh,
        in_specs=placed,
        out_specs=P("sub", "coarse", None, None),
        check_vma=False,
    )
```

profile of v0, /device:TPU:0, one launch (start us, length us, event | category | flops | bytes accessed | tf_op | source)
XLA Modules:
  0.0 958.9 jit_solution(15861982066872133460)
XLA Ops:
  2.3 42.2 %psum.91 = f32[]{:T(128)} all-reduce(f32[]{:T(128)} %multiply_reduce_fusion.14), channel_id=1, replica_groups=mesh['sub'=8,'coarse'=4] {'sub','coarse'}, use_global_device_ids=true, to_apply=%region_1.0 | all-reduce | flops 1 | bytes 8 | tf_op jit(solution)/shard_map/psum | solution.py:94
  46.9 10.0 %all_gather.108 = f32[64,128]{1,0:T(8,128)S(1)} all-gather(f32[8,128]{1,0:T(8,128)S(1)} %get-tuple-element.63), channel_id=1, replica_groups=mesh['sub'=8,'coarse'=4] {'sub'}, dimensions={0}, use_global_device_ids=true | all-gather | bytes 36864 | tf_op jit(solution)/shard_map/all_gather | solution.py:82
  59.0 8.1 all_gather.109
  67.9 9.1 all_gather.110
  77.6 8.1 all_gather.111
  87.8 15.4 %fusion.6 = f32[128,1,128]{2,1,0:T(1,128)S(1)} fusion(f32[128,128,1]{1,2,0:T(1,128)S(1)} %bitcast.355, f32[1,1,128,128,128]{4,3,2,1,0:T(8,128)} %param.16), kind=kOutput, calls=%fused_computation.14 | convolution fusion | flops 25165824 | bytes 8519680 | tf_op jit(solution)/shard_map/bij,bj->bi/dot_general | solution.py:107
  103.5 39.4 %psum.92 = f32[512]{0:T(512)S(1)} all-reduce(f32[512]{0:T(512)S(1)} %broadcast_multiply_fusion.3), channel_id=1, replica_groups=mesh['sub'=8,'coarse'=4] {'sub','coarse'}, use_global_device_ids=true, to_apply=%region_3.5 | all-reduce | flops 512 | bytes 4096 | tf_op jit(solution)/shard_map/psum | solution.py:104
  143.1 9.8 %all-gather = f32[4,1,128]{2,1,0:T(1,128)S(1)} all-gather(f32[1,1,128]{2,1,0:T(1,128)S(1)} %convolution_bitcast_fusion.7), channel_id=1, replica_groups=mesh['sub'=8,'coarse'=4] {'coarse'}, dimensions={0}, use_global_device_ids=true | all-gather | bytes 2560 | tf_op jit(solution)/shard_map/all_gather | solution.py:111
  153.9 9.8 %all_gather.113 = f32[64,128]{1,0:T(8,128)S(1)} all-gather(f32[8,128]{1,0:T(8,128)S(1)} %get-tuple-element.59), channel_id=1, replica_groups=mesh['sub'=8,'coarse'=4] {'sub'}, dimensions={0}, use_global_device_ids=true | all-gather | bytes 36864 | tf_op jit(solution)/shard_map/all_gather | solution.py:82
  163.8 9.1 all_gather.114
  180.9 9.1 all_gather.116
  191.5 37.8 %psum.93 = f32[]{:T(128)} all-reduce(f32[]{:T(128)} %get-tuple-element.80), channel_id=1, replica_groups=mesh['sub'=8,'coarse'=4] {'sub','coarse'}, use_global_device_ids=true, to_apply=%region_5.7 | all-reduce | flops 1 | bytes 8 | tf_op jit(solution)/shard_map/psum | solution.py:125
  230.6 41.2 %psum.94 = f32[]{:T(128)} all-reduce(f32[]{:T(128)} %multiply_reduce_fusion.12), channel_id=1, replica_groups=mesh['sub'=8,'coarse'=4] {'sub','coarse'}, use_global_device_ids=true, to_apply=%region_7.9 | all-reduce | flops 1 | bytes 8 | tf_op jit(solution)/shard_map/psum | solution.py:94
  274.0 10.1 %all_gather.117 = f32[64,128]{1,0:T(8,128)S(1)} all-gather(f32[8,128]{1,0:T(8,128)S(1)} %get-tuple-element.55), channel_id=1, replica_groups=mesh['sub'=8,'coarse'=4] {'sub'}, dimensions={0}, use_global_device_ids=true | all-gather | bytes 36864 | tf_op jit(solution)/shard_map/all_gather | solution.py:82
  284.1 9.0 all_gather.118
  301.2 9.0 all_gather.120
  311.1 15.4 %fusion.4 = f32[128,1,128]{2,1,0:T(1,128)S(1)} fusion(f32[128,128,1]{1,2,0:T(1,128)S(1)} %bitcast.356, f32[1,1,128,128,128]{4,3,2,1,0:T(8,128)} %param.16), kind=kOutput, calls=%fused_computation.12 | convolution fusion | flops 25165824 | bytes 8519680 | tf_op jit(solution)/shard_map/bij,bj->bi/dot_general | solution.py:107
  326.8 37.7 %psum.95 = f32[512]{0:T(512)S(1)} all-reduce(f32[512]{0:T(512)S(1)} %broadcast_multiply_fusion.2), channel_id=1, replica_groups=mesh['sub'=8,'coarse'=4] {'sub','coarse'}, use_global_device_ids=true, to_apply=%region_9.11 | all-reduce | flops 512 | bytes 4096 | tf_op jit(solution)/shard_map/psum | solution.py:104
  364.7 9.6 %all-gather.1 = f32[4,1,128]{2,1,0:T(1,128)S(1)} all-gather(f32[1,1,128]{2,1,0:T(1,128)S(1)} %convolution_bitcast_fusion.5), channel_id=1, replica_groups=mesh['sub'=8,'coarse'=4] {'coarse'}, dimensions={0}, use_global_device_ids=true | all-gather | bytes 2560 | tf_op jit(solution)/shard_map/all_gather | solution.py:111
  375.4 9.8 %all_gather.122 = f32[64,128]{1,0:T(8,128)S(1)} all-gather(f32[8,128]{1,0:T(8,128)S(1)} %get-tuple-element.51), channel_id=1, replica_groups=mesh['sub'=8,'coarse'=4] {'sub'}, dimensions={0}, use_global_device_ids=true | all-gather | bytes 36864 | tf_op jit(solution)/shard_map/all_gather | solution.py:82
  393.3 9.0 all_gather.124
  402.3 8.3 all_gather.125
  413.5 37.6 %psum.96 = f32[2]{0:T(128)S(1)} all-reduce(f32[2]{0:T(128)S(1)} %pad_maximum_fusion.8), channel_id=1, replica_groups=mesh['sub'=8,'coarse'=4] {'sub','coarse'}, use_global_device_ids=true, to_apply=%region_12.14 | all-reduce | flops 2 | bytes 16 | tf_op jit(solution)/shard_map/psum | solution.py:125
  453.6 41.7 %psum.97 = f32[]{:T(128)} all-reduce(f32[]{:T(128)} %get-tuple-element.21), channel_id=1, replica_groups=mesh['sub'=8,'coarse'=4] {'sub','coarse'}, use_global_device_ids=true, to_apply=%region_14.16 | all-reduce | flops 1 | bytes 8 | tf_op jit(solution)/shard_map/psum | solution.py:94
  496.8 10.1 %all_gather.126 = f32[64,128]{1,0:T(8,128)S(1)} all-gather(f32[8,128]{1,0:T(8,128)S(1)} %get-tuple-element.47), channel_id=1, replica_groups=mesh['sub'=8,'coarse'=4] {'sub'}, dimensions={0}, use_global_device_ids=true | all-gather | bytes 36864 | tf_op jit(solution)/shard_map/all_gather | solution.py:82
  506.9 8.1 all_gather.127
  515.0 9.0 all_gather.128
  524.0 8.1 all_gather.129
  533.0 15.4 %fusion.2 = f32[128,1,128]{2,1,0:T(1,128)S(1)} fusion(f32[128,128,1]{1,2,0:T(1,128)S(1)} %bitcast.357, f32[1,1,128,128,128]{4,3,2,1,0:T(8,128)} %param.16), kind=kOutput, calls=%fused_computation.10 | convolution fusion | flops 25165824 | bytes 8519680 | tf_op jit(solution)/shard_map/bij,bj->bi/dot_general | solution.py:107
  548.6 37.7 %psum.98 = f32[512]{0:T(512)S(1)} all-reduce(f32[512]{0:T(512)S(1)} %broadcast_multiply_fusion.1), channel_id=1, replica_groups=mesh['sub'=8,'coarse'=4] {'sub','coarse'}, use_global_device_ids=true, to_apply=%region_16.18 | all-reduce | flops 512 | bytes 4096 | tf_op jit(solution)/shard_map/psum | solution.py:104
  586.5 9.6 %all-gather.2 = f32[4,1,128]{2,1,0:T(1,128)S(1)} all-gather(f32[1,1,128]{2,1,0:T(1,128)S(1)} %convolution_bitcast_fusion.3), channel_id=1, replica_groups=mesh['sub'=8,'coarse'=4] {'coarse'}, dimensions={0}, use_global_device_ids=true | all-gather | bytes 2560 | tf_op jit(solution)/shard_map/all_gather | solution.py:111
  597.2 9.8 %all_gather.131 = f32[64,128]{1,0:T(8,128)S(1)} all-gather(f32[8,128]{1,0:T(8,128)S(1)} %get-tuple-element.43), channel_id=1, replica_groups=mesh['sub'=8,'coarse'=4] {'sub'}, dimensions={0}, use_global_device_ids=true | all-gather | bytes 36864 | tf_op jit(solution)/shard_map/all_gather | solution.py:82
  607.0 9.0 all_gather.132
  616.1 8.5 all_gather.133
  624.6 9.0 all_gather.134
  637.2 37.6 %psum.99 = f32[3]{0:T(128)S(1)} all-reduce(f32[3]{0:T(128)S(1)} %pad_maximum_fusion.9), channel_id=1, replica_groups=mesh['sub'=8,'coarse'=4] {'sub','coarse'}, use_global_device_ids=true, to_apply=%region_20.22 | all-reduce | flops 3 | bytes 24 | tf_op jit(solution)/shard_map/psum | solution.py:125
  677.9 40.7 %psum.100 = f32[]{:T(128)} all-reduce(f32[]{:T(128)} %get-tuple-element.17), channel_id=1, replica_groups=mesh['sub'=8,'coarse'=4] {'sub','coarse'}, use_global_device_ids=true, to_apply=%region_22.24 | all-reduce | flops 1 | bytes 8 | tf_op jit(solution)/shard_map/psum | solution.py:94
  720.0 10.0 %all_gather.135 = f32[64,128]{1,0:T(8,128)S(1)} all-gather(f32[8,128]{1,0:T(8,128)S(1)} %get-tuple-element.39), channel_id=1, replica_groups=mesh['sub'=8,'coarse'=4] {'sub'}, dimensions={0}, use_global_device_ids=true | all-gather | bytes 36864 | tf_op jit(solution)/shard_map/all_gather | solution.py:82
  730.0 9.0 all_gather.136
  747.1 9.0 all_gather.138
  757.1 15.4 %fusion = f32[128,1,128]{2,1,0:T(1,128)S(1)} fusion(f32[128,128,1]{1,2,0:T(1,128)S(1)} %bitcast.358, f32[1,1,128,128,128]{4,3,2,1,0:T(8,128)} %param.16), kind=kOutput, calls=%fused_computation.8 | convolution fusion | flops 25165824 | bytes 8519680 | tf_op jit(solution)/shard_map/bij,bj->bi/dot_general | solution.py:107
  772.7 37.7 %psum.101 = f32[512]{0:T(512)S(1)} all-reduce(f32[512]{0:T(512)S(1)} %broadcast_multiply_fusion), channel_id=1, replica_groups=mesh['sub'=8,'coarse'=4] {'sub','coarse'}, use_global_device_ids=true, to_apply=%region_24.26 | all-reduce | flops 512 | bytes 4096 | tf_op jit(solution)/shard_map/psum | solution.py:104
  810.6 9.6 %all-gather.3 = f32[4,1,128]{2,1,0:T(1,128)S(1)} all-gather(f32[1,1,128]{2,1,0:T(1,128)S(1)} %convolution_bitcast_fusion.1), channel_id=1, replica_groups=mesh['sub'=8,'coarse'=4] {'coarse'}, dimensions={0}, use_global_device_ids=true | all-gather | bytes 2560 | tf_op jit(solution)/shard_map/all_gather | solution.py:111
  821.3 9.8 %all_gather.140 = f32[64,128]{1,0:T(8,128)S(1)} all-gather(f32[8,128]{1,0:T(8,128)S(1)} %get-tuple-element.35), channel_id=1, replica_groups=mesh['sub'=8,'coarse'=4] {'sub'}, dimensions={0}, use_global_device_ids=true | all-gather | bytes 36864 | tf_op jit(solution)/shard_map/all_gather | solution.py:82
  831.1 8.2 all_gather.141
  839.4 9.0 all_gather.142
  860.6 37.6 %psum.102 = f32[4]{0:T(128)S(1)} all-reduce(f32[4]{0:T(128)S(1)} %pad_maximum_fusion.10), channel_id=1, replica_groups=mesh['sub'=8,'coarse'=4] {'sub','coarse'}, use_global_device_ids=true, to_apply=%region_29.31 | all-reduce | flops 4 | bytes 32 | tf_op jit(solution)/shard_map/psum | solution.py:125
  908.5 41.8 %psum.103 = f32[]{:T(128)} all-reduce(f32[]{:T(128)} %multiply_reduce_fusion), channel_id=1, replica_groups=mesh['sub'=8,'coarse'=4] {'sub','coarse'}, use_global_device_ids=true, to_apply=%region_31.33 | all-reduce | flops 1 | bytes 8 | tf_op jit(solution)/shard_map/psum | solution.py:94
  (135 shorter events, 82.6 us)
Async XLA Ops:
  0.0 87.0 %copy-start = (f32[1,1,4,128,128]{4,3,2,1,0:T(8,128)S(1)}, f32[1,1,4,128,128]{4,3,2,1,0:T(8,128)}, u32[]{:S(2)}) copy-start(f32[1,1,4,128,128]{4,3,2,1,0:T(8,128)} %param.17) | copy-start | bytes 786436
  0.0 153.1 %copy-start.1 = (f32[1,1,128,128]{3,2,1,0:T(8,128)S(1)}, f32[1,1,128,128]{3,2,1,0:T(8,128)}, u32[]{:S(2)}) copy-start(f32[1,1,128,128]{3,2,1,0:T(8,128)} %param.18) | copy-start | bytes 196612
  0.0 103.2 %copy-start.5 = (s32[1,1,128]{2,1,0:T(1,128)S(1)}, s32[1,1,128]{2,1,0:T(1,128)}, u32[]{:S(2)}) copy-start(s32[1,1,128]{2,1,0:T(1,128)} %param.23) | copy-start | bytes 1540
  0.0 142.9 %copy-start.2 = (f32[128,512]{1,0:T(8,128)S(1)}, f32[128,512]{1,0:T(8,128)}, u32[]{:S(2)}) copy-start(f32[128,512]{1,0:T(8,128)} %param.19) | copy-start | bytes 786436
  0.0 190.4 %copy-start.3 = (f32[1,1,128,128]{3,2,1,0:T(8,128)S(1)}, f32[1,1,128,128]{3,2,1,0:T(8,128)}, u32[]{:S(2)}) copy-start(f32[1,1,128,128]{3,2,1,0:T(8,128)} %param.15) | copy-start | bytes 196612
  0.0 190.5 %copy-start.4 = (f32[1,1,128,128]{3,2,1,0:T(8,128)S(1)}, f32[1,1,128,128]{3,2,1,0:T(8,128)}, u32[]{:S(2)}) copy-start(f32[1,1,128,128]{3,2,1,0:T(8,128)} %param.14) | copy-start | bytes 196612
where the time goes:
time: 971 us; the launch traced here: 959 us
  blocking collectives  835 us (86%)
  matrix products  73.9 us (8%)
  other arithmetic  21.1 us (2%)
  between operations  20.1 us (2%)
    all_gather x32, blocking collectives, margin(): gathered = lax.all_gather(outgoing[round_id], 'sub', axis=0, tiled=True)  286 us
    psum x5, blocking collectives, squared_norm(): return lax.psum(jnp.sum(values * values), ('sub', 'coarse'))  208 us
    psum x4, blocking collectives, on_device(): lax.psum(jnp.dot(inner, member_table, precision=highest) * factor, ('sub'...  152 us
    psum x4, blocking collectives, on_device(): lax.psum(jnp.stack([jnp.sum(vector * product) for vector in basis_list]),...  151 us
    dot_general x4, matrix products, on_device(): jnp.einsum('bij,bj->bi', inverse_blocks, current + margin(current), preci...  61.5 us
    all_gather x4, blocking collectives, on_device(): coarse_full = lax.all_gather(coarse_part, 'coarse', axis=0, tiled=True)  38.7 us

commit v1 on v0

--- a/solution.py
+++ b/solution.py
@@ -101,9 +101,9 @@
     for krylov_step in range(ITERS):
         current = basis_list[-1]
         inner = jnp.sum(basis_local * current, axis=1)
-        restricted = lax.psum(
-            jnp.dot(inner, member_table, precision=highest) * factor, ("sub", "coarse")
-        )
+        part = jnp.dot(inner, member_table, precision=highest) * factor
+        parts = lax.all_gather(part, ("sub", "coarse"), axis=0, tiled=False)
+        restricted = parts.sum(axis=0)
         local_part = jnp.einsum(
             "bij,bj->bi", inverse_blocks, current + margin(current), precision=highest
         )

time: 971 us -> 1070 us (1.10)
  blocking collectives: 835 us -> 936 us
    all_gather x0 -> x4, blocking collectives: none -> 267 us  [on_device(): parts = lax.all_gather(part, ('sub', 'coarse'), axis=0, tiled=False)]
    psum x4 -> x0, blocking collectives: 152 us -> none  [on_device(): lax.psum(jnp.dot(inner, member_table, precision=highest) * factor, ('sub'...]
where the time goes in v1:
time: 1070 us; the launch traced here: 1060 us
  blocking collectives  936 us (87%)
  matrix products  73.9 us (7%)
  other arithmetic  21.3 us (2%)
  between operations  20.1 us (2%)
    all_gather x32, blocking collectives, margin(): gathered = lax.all_gather(outgoing[round_id], 'sub', axis=0, tiled=True)  278 us
    all_gather x4, blocking collectives, on_device(): parts = lax.all_gather(part, ('sub', 'coarse'), axis=0, tiled=False)  267 us
    psum x5, blocking collectives, squared_norm(): return lax.psum(jnp.sum(values * values), ('sub', 'coarse'))  201 us
    psum x4, blocking collectives, on_device(): lax.psum(jnp.stack([jnp.sum(vector * product) for vector in basis_list]),...  160 us
    dot_general x4, matrix products, on_device(): jnp.einsum('bij,bj->bi', inverse_blocks, current + margin(current), preci...  61.5 us
    all_gather x4, blocking collectives, on_device(): coarse_full = lax.all_gather(coarse_part, 'coarse', axis=0, tiled=True)  30.2 us

profile of v1, /device:TPU:0, one launch (start us, length us, event | category | flops | bytes accessed | tf_op | source)
XLA Modules:
  0.0 1060.0 jit_solution(2502491910254648364)
XLA Ops:
  2.3 42.2 %psum.63 = f32[]{:T(128)} all-reduce(f32[]{:T(128)} %multiply_reduce_fusion.14), channel_id=1, replica_groups=mesh['sub'=8,'coarse'=4] {'sub','coarse'}, use_global_device_ids=true, to_apply=%region_1.0 | all-reduce | flops 1 | bytes 8 | tf_op jit(solution)/shard_map/psum | solution.py:94
  46.9 10.0 all_gather.132
  59.0 8.1 all_gather.133
  67.9 9.1 all_gather.134
  87.8 15.4 %fusion.6 = f32[128,1,128]{2,1,0:T(1,128)S(1)} fusion(f32[128,128,1]{1,2,0:T(1,128)S(1)} %bitcast.359, f32[1,1,128,128,128]{4,3,2,1,0:T(8,128)} %param.16), kind=kOutput, calls=%fused_computation.14 | convolution fusion | flops 25165824 | bytes 8519680 | tf_op jit(solution)/shard_map/bij,bj->bi/dot_general | solution.py:107
  103.5 66.8 %all-gather.4 = f32[32,1,512]{2,1,0:T(1,128)S(1)} all-gather(f32[1,1,512]{2,1,0:T(1,128)S(1)} %bitcast.367), channel_id=2, replica_groups=mesh['sub'=8,'coarse'=4] {'sub','coarse'}, dimensions={0}, use_global_device_ids=true | all-gather | bytes 67584 | tf_op jit(solution)/shard_map/all_gather | solution.py:105
  179.3 9.0 all_gather.139
  188.3 8.1 all_gather.140
  196.4 9.0 all_gather.141
  205.4 8.1 all_gather.142
  215.1 40.1 %psum.64 = f32[]{:T(128)} all-reduce(f32[]{:T(128)} %get-tuple-element.80), channel_id=1, replica_groups=mesh['sub'=8,'coarse'=4] {'sub','coarse'}, use_global_device_ids=true, to_apply=%region_5.7 | all-reduce | flops 1 | bytes 8 | tf_op jit(solution)/shard_map/psum | solution.py:125
  256.5 39.8 %psum.65 = f32[]{:T(128)} all-reduce(f32[]{:T(128)} %multiply_reduce_fusion.12), channel_id=1, replica_groups=mesh['sub'=8,'coarse'=4] {'sub','coarse'}, use_global_device_ids=true, to_apply=%region_7.9 | all-reduce | flops 1 | bytes 8 | tf_op jit(solution)/shard_map/psum | solution.py:94
  298.5 10.1 all_gather.143
  308.6 8.1 all_gather.144
  316.7 9.0 all_gather.145
  325.7 8.1 all_gather.146
  334.7 15.4 %fusion.4 = f32[128,1,128]{2,1,0:T(1,128)S(1)} fusion(f32[128,128,1]{1,2,0:T(1,128)S(1)} %bitcast.360, f32[1,1,128,128,128]{4,3,2,1,0:T(8,128)} %param.16), kind=kOutput, calls=%fused_computation.12 | convolution fusion | flops 25165824 | bytes 8519680 | tf_op jit(solution)/shard_map/bij,bj->bi/dot_general | solution.py:107
  350.4 66.7 %all-gather.6 = f32[32,1,512]{2,1,0:T(1,128)S(1)} all-gather(f32[1,1,512]{2,1,0:T(1,128)S(1)} %bitcast.368), channel_id=3, replica_groups=mesh['sub'=8,'coarse'=4] {'sub','coarse'}, dimensions={0}, use_global_device_ids=true | all-gather | bytes 67584 | tf_op jit(solution)/shard_map/all_gather | solution.py:105
  426.0 8.9 all_gather.150
  435.0 8.2 all_gather.151
  443.2 8.9 all_gather.152
  452.1 8.2 all_gather.153
  463.2 40.1 %psum.66 = f32[2]{0:T(128)S(1)} all-reduce(f32[2]{0:T(128)S(1)} %pad_maximum_fusion.8), channel_id=1, replica_groups=mesh['sub'=8,'coarse'=4] {'sub','coarse'}, use_global_device_ids=true, to_apply=%region_12.14 | all-reduce | flops 2 | bytes 16 | tf_op jit(solution)/shard_map/psum | solution.py:125
  505.8 39.5 %psum.67 = f32[]{:T(128)} all-reduce(f32[]{:T(128)} %get-tuple-element.21), channel_id=1, replica_groups=mesh['sub'=8,'coarse'=4] {'sub','coarse'}, use_global_device_ids=true, to_apply=%region_14.16 | all-reduce | flops 1 | bytes 8 | tf_op jit(solution)/shard_map/psum | solution.py:94
  546.8 10.1 all_gather.154
  556.9 8.2 all_gather.155
  565.1 8.9 all_gather.156
  574.0 8.2 all_gather.157
  583.0 15.4 %fusion.2 = f32[128,1,128]{2,1,0:T(1,128)S(1)} fusion(f32[128,128,1]{1,2,0:T(1,128)S(1)} %bitcast.361, f32[1,1,128,128,128]{4,3,2,1,0:T(8,128)} %param.16), kind=kOutput, calls=%fused_computation.10 | convolution fusion | flops 25165824 | bytes 8519680 | tf_op jit(solution)/shard_map/bij,bj->bi/dot_general | solution.py:107
  598.7 66.7 %all-gather.8 = f32[32,1,512]{2,1,0:T(1,128)S(1)} all-gather(f32[1,1,512]{2,1,0:T(1,128)S(1)} %bitcast.369), channel_id=4, replica_groups=mesh['sub'=8,'coarse'=4] {'sub','coarse'}, dimensions={0}, use_global_device_ids=true | all-gather | bytes 67584 | tf_op jit(solution)/shard_map/all_gather | solution.py:105
  674.3 9.0 all_gather.161
  683.3 8.1 all_gather.162
  691.4 9.0 all_gather.163
  700.4 8.1 all_gather.164
  712.1 39.9 %psum.68 = f32[3]{0:T(128)S(1)} all-reduce(f32[3]{0:T(128)S(1)} %pad_maximum_fusion.9), channel_id=1, replica_groups=mesh['sub'=8,'coarse'=4] {'sub','coarse'}, use_global_device_ids=true, to_apply=%region_20.22 | all-reduce | flops 3 | bytes 24 | tf_op jit(solution)/shard_map/psum | solution.py:125
  755.1 39.5 %psum.69 = f32[]{:T(128)} all-reduce(f32[]{:T(128)} %get-tuple-element.17), channel_id=1, replica_groups=mesh['sub'=8,'coarse'=4] {'sub','coarse'}, use_global_device_ids=true, to_apply=%region_22.24 | all-reduce | flops 1 | bytes 8 | tf_op jit(solution)/shard_map/psum | solution.py:94
  796.0 10.0 all_gather.165
  806.0 8.1 all_gather.166
  814.2 9.0 all_gather.167
  823.2 8.1 all_gather.168
  832.1 15.4 %fusion = f32[128,1,128]{2,1,0:T(1,128)S(1)} fusion(f32[128,128,1]{1,2,0:T(1,128)S(1)} %bitcast.362, f32[1,1,128,128,128]{4,3,2,1,0:T(8,128)} %param.16), kind=kOutput, calls=%fused_computation.8 | convolution fusion | flops 25165824 | bytes 8519680 | tf_op jit(solution)/shard_map/bij,bj->bi/dot_general | solution.py:107
  847.8 66.7 %all-gather.10 = f32[32,1,512]{2,1,0:T(1,128)S(1)} all-gather(f32[1,1,512]{2,1,0:T(1,128)S(1)} %bitcast.370), channel_id=5, replica_groups=mesh['sub'=8,'coarse'=4] {'sub','coarse'}, dimensions={0}, use_global_device_ids=true | all-gather | bytes 67584 | tf_op jit(solution)/shard_map/all_gather | solution.py:105
  923.5 8.9 all_gather.172
  932.4 8.2 all_gather.173
  940.6 8.9 all_gather.174
  949.5 8.2 all_gather.175
  961.9 39.7 %psum.70 = f32[4]{0:T(128)S(1)} all-reduce(f32[4]{0:T(128)S(1)} %pad_maximum_fusion.10), channel_id=1, replica_groups=mesh['sub'=8,'coarse'=4] {'sub','coarse'}, use_global_device_ids=true, to_apply=%region_29.31 | all-reduce | flops 4 | bytes 32 | tf_op jit(solution)/shard_map/psum | solution.py:125
  1011.8 39.5 %psum.71 = f32[]{:T(128)} all-reduce(f32[]{:T(128)} %multiply_reduce_fusion), channel_id=1, replica_groups=mesh['sub'=8,'coarse'=4] {'sub','coarse'}, use_global_device_ids=true, to_apply=%region_31.33 | all-reduce | flops 1 | bytes 8 | tf_op jit(solution)/shard_map/psum | solution.py:94
  (139 shorter events, 80.9 us)
Async XLA Ops:
  0.0 87.0 %copy-start = (f32[1,1,4,128,128]{4,3,2,1,0:T(8,128)S(1)}, f32[1,1,4,128,128]{4,3,2,1,0:T(8,128)}, u32[]{:S(2)}) copy-start(f32[1,1,4,128,128]{4,3,2,1,0:T(8,128)} %param.17) | copy-start | bytes 786436
  0.0 178.4 %copy-start.1 = (f32[1,1,128,128]{3,2,1,0:T(8,128)S(1)}, f32[1,1,128,128]{3,2,1,0:T(8,128)}, u32[]{:S(2)}) copy-start(f32[1,1,128,128]{3,2,1,0:T(8,128)} %param.18) | copy-start | bytes 196612
  0.0 103.2 %copy-start.5 = (s32[1,1,128]{2,1,0:T(1,128)S(1)}, s32[1,1,128]{2,1,0:T(1,128)}, u32[]{:S(2)}) copy-start(s32[1,1,128]{2,1,0:T(1,128)} %param.23) | copy-start | bytes 1540
  0.0 170.4 %copy-start.2 = (f32[128,512]{1,0:T(8,128)S(1)}, f32[128,512]{1,0:T(8,128)}, u32[]{:S(2)}) copy-start(f32[128,512]{1,0:T(8,128)} %param.19) | copy-start | bytes 786436
  0.0 214.0 %copy-start.3 = (f32[1,1,128,128]{3,2,1,0:T(8,128)S(1)}, f32[1,1,128,128]{3,2,1,0:T(8,128)}, u32[]{:S(2)}) copy-start(f32[1,1,128,128]{3,2,1,0:T(8,128)} %param.15) | copy-start | bytes 196612
  0.0 214.1 %copy-start.4 = (f32[1,1,128,128]{3,2,1,0:T(8,128)S(1)}, f32[1,1,128,128]{3,2,1,0:T(8,128)}, u32[]{:S(2)}) copy-start(f32[1,1,128,128]{3,2,1,0:T(8,128)} %param.14) | copy-start | bytes 196612
